TPU v7x, 256 devices: a whole 4x4x8 slice. The times are simulated.
256 devices in a mesh: tm: 8 (over z), height: 16 (over x, y), width: 2 (over core).
Axes of the slice: x: 4, y: 4, z: 8, core: 2. Of those that a mesh axis runs over, the one named last changes fastest.
Arguments:
- video: bfloat16 [2, 128, 16, 256, 128], P('width', ('tm', 'height')), may hold values from -6 to 6
- out_grad: bfloat16 [2, 128, 16, 256, 128], P('width', None, 'tm', 'height'), may hold values from -6 to 6
- lengths: int32 [4], replicated, may hold values from 1 to 6, 16 in all
- temporal_weight: bfloat16 [3, 128, 128], replicated, may hold values from -0.3125 to 0.3125
- spatial_weight: bfloat16 [3, 3, 128, 128], replicated, may hold values from -0.1875 to 0.1875
Outputs:
- video_grad: bfloat16 [2, 128, 16, 256, 128], P('width', ('tm', 'height'))
- temporal_grad: float32 [3, 128, 128], replicated
- spatial_grad: float32 [3, 3, 128, 128], replicated
Inputs may be any that keep to these rules, and one draw needn't show every extreme that they name: The 4 clips lie end to end in frame order, their lengths sum to 16, and the longest clip has exactly 6 frames.
All inputs are finite; a program needn't handle non-finite values.
Results may differ from a plain program's by a relative error of at most 0.008.
Values may be sent and summed in bfloat16 or wider, within the bound.
A program may use at most 128 MiB of HBM per device.

v0:
```python
import jax
import jax.numpy as jnp
from jax import lax
from jax.sharding import PartitionSpec as P


def with_halo(cells, sides, width):
    for axis, dim in sides:
        count = lax.axis_size(axis)
        ends = count - 1
        head = lax.slice_in_dim(cells, 0, width, axis=dim)
        tail = lax.slice_in_dim(cells, cells.shape[dim] - width, cells.shape[dim], axis=dim)
        cells = jnp.concatenate(
            [
                lax.ppermute(tail, axis, [(i, (i + 1) % count) for i in range(ends)]),
                cells,
                lax.ppermute(head, axis, [((i + 1) % count, i) for i in range(ends)]),
            ],
            axis=dim,
        )
    return cells


def frame_masks(lengths, frames):
    ends = jnp.cumsum(lengths, dtype=jnp.int32)
    starts = ends - lengths
    frame_index = jnp.arange(frames, dtype=jnp.int32)
    inside = (frame_index[:, None] >= starts[None, :]) & (frame_index[:, None] < ends[None, :])
    first = jnp.sum(jnp.where(inside, starts[None, :], 0), axis=1, dtype=jnp.int32)
    return jnp.stack([frame_index - lag >= first for lag in range(3)]).astype(jnp.bfloat16)


def silu_slope(pre, grads):
    sig = jax.nn.sigmoid(pre)
    return grads.astype(jnp.float32) * sig * (1.0 + pre * (1.0 - sig))


def flatten(block):
    return block.reshape(-1, block.shape[-1])


def spatial_forward(padded, weights, cols, rows):
    total = None
    for row_off in range(3):
        for col_off in range(3):
            piece = flatten(padded[col_off : col_off + cols, :, row_off : row_off + rows])
            term = jnp.dot(piece, weights[row_off, col_off], preferred_element_type=jnp.float32)
            total = term if total is None else total + term
    return total


def shards(video, out_grad, lengths, temporal_weight, spatial_weight):
    width_loc = video.shape[1]
    frames = video.shape[2]
    rows = video.shape[3]
    chans = video.shape[4]
    n_tm = lax.axis_size("tm")
    n_height = lax.axis_size("height")
    frames_dev = frames // n_tm
    rows_dev = rows // n_height
    cols_half = out_grad.shape[1]
    total_cols = cols_half * lax.axis_size("width")
    masks = frame_masks(lengths, frames)
    local_video = video[0]
    padded_video = jnp.pad(local_video, ((0, 0), (2, 0), (0, 0), (0, 0)))
    taps = [
        padded_video[:, 2 - lag : 2 - lag + frames] * masks[lag][None, :, None, None]
        for lag in range(3)
    ]
    total = None
    for lag in range(3):
        term = jnp.dot(flatten(taps[lag]), temporal_weight[lag], preferred_element_type=jnp.float32)
        total = term if total is None else total + term
    act_time = total.astype(jnp.bfloat16).reshape(local_video.shape)
    arranged = act_time.reshape(width_loc, n_tm, frames_dev, n_height, rows_dev, chans)
    arranged = arranged.transpose(1, 3, 0, 2, 4, 5).reshape(
        n_tm * n_height * width_loc, frames_dev, rows_dev, chans
    )
    act_space = lax.all_to_all(arranged, ("tm", "height"), split_axis=0, concat_axis=0, tiled=True)
    grad_space = out_grad[0]
    padded_act = with_halo(act_space, (("height", 2), ("width", 0)), 1)
    pre = spatial_forward(padded_act, spatial_weight, cols_half, rows_dev)
    delta = silu_slope(pre, flatten(grad_space)).astype(jnp.bfloat16).reshape(act_space.shape)
    padded_delta = with_halo(delta, (("height", 2), ("width", 0)), 1)
    flat_delta = flatten(delta)
    back = None
    spatial_terms = []
    for row_off in range(3):
        line = []
        for col_off in range(3):
            piece = flatten(
                padded_delta[
                    2 - col_off : 2 - col_off + cols_half, :, 2 - row_off : 2 - row_off + rows_dev
                ]
            )
            term = jnp.dot(
                piece, spatial_weight[row_off, col_off].T, preferred_element_type=jnp.float32
            )
            back = term if back is None else back + term
            source = flatten(
                padded_act[col_off : col_off + cols_half, :, row_off : row_off + rows_dev]
            )
            line.append(
                lax.dot_general(
                    source, flat_delta, (((0,), (0,)), ((), ())), preferred_element_type=jnp.float32
                )
            )
        spatial_terms.append(jnp.stack(line))
    spatial_local = jnp.stack(spatial_terms)
    grad_act_space = back.astype(jnp.bfloat16).reshape(act_space.shape)
    received = lax.all_to_all(
        grad_act_space, ("tm", "height"), split_axis=0, concat_axis=0, tiled=True
    )
    received = received.reshape(n_tm, n_height, width_loc, frames_dev, rows_dev, chans)
    grad_time = received.transpose(2, 0, 3, 1, 4, 5).reshape(width_loc, frames, rows, chans)
    flat_grad = flatten(grad_time)
    frame_total = None
    temporal_terms = []
    for lag in range(3):
        temporal_terms.append(
            lax.dot_general(
                flatten(taps[lag]),
                flat_grad,
                (((0,), (0,)), ((), ())),
                preferred_element_type=jnp.float32,
            )
        )
        masked = flatten(grad_time * masks[lag][None, :, None, None])
        product = jnp.dot(
            masked, temporal_weight[lag].T, preferred_element_type=jnp.float32
        ).reshape(grad_time.shape)
        moved = jnp.pad(product[:, lag:], ((0, 0), (0, lag), (0, 0), (0, 0)))
        frame_total = moved if frame_total is None else frame_total + moved
    temporal_local = jnp.stack(temporal_terms)
    video_grad = frame_total.astype(jnp.bfloat16)[None]
    scale = float(frames * rows * total_cols) ** (-0.5)
    temporal_grad, spatial_grad = lax.psum(
        (temporal_local * scale, spatial_local * scale), ("tm", "height", "width")
    )
    return (video_grad, temporal_grad, spatial_grad)


def solution(mesh):
    placed = (
        P("width", ("tm", "height"), None, None, None),
        P("width", None, "tm", "height", None),
        P(),
        P(),
        P(),
    )
    return jax.shard_map(
        shards,
        mesh=mesh,
        in_specs=placed,
        out_specs=(P("width", ("tm", "height"), None, None, None), P(), P()),
        check_vma=False,
    )
```

profile of v0, /device:TPU:2, one launch (start us, length us, event | category | flops | bytes accessed | tf_op | source)
XLA Modules:
  0.0 414.0 jit_solution(14738831127467204281)
XLA Ops:
  8.8 1.4 broadcast_multiply_fusion
  14.0 46.1 %all_to_all.10 = bf16[128,2,16,128]{3,2,1,0:T(8,128)(2,1)S(1)} all-to-all(bf16[128,2,16,128]{3,2,1,0:T(8,128)(2,1)S(1)} %bitcast.249), channel_id=1, replica_groups=mesh['tm'=8,'height'=16,'width'=2] {'tm','height'}, dimensions={0} | all-to-all | bytes 2097152 | tf_op jit(solution)/shard_map/all_to_all | solution.py:79
  60.2 2.4 collective-permute-start
  62.7 5.5 %collective-permute-start.1 = (bf16[128,2,1,128]{3,2,1,0:T(2,128)(2,1)S(1)}, bf16[128,2,1,128]{3,2,1,0:T(2,128)(2,1)S(1)}, u32[]{:S(2)}, u32[]{:S(2)}) collective-permute-start(bf16[128,2,1,128]{3,2,1,0:T(2,128)(2,1)S(1)} %get-tuple-element.38), channel_id=1, source_target_pairs={{2,0},{4,2},{6,4},{8,6},{10,8},{12,10},{14,12},{16,14},{18,16},{20... | collective-permute-start | bytes 196616 | tf_op jit(solution)/shard_map/ppermute | solution.py:17
  69.2 1.5 collective-permute-done.1
  75.1 2.0 maximum_maximum_fusion
  77.1 1.3 fusion.67
  84.4 1.9 collective-permute-start.4
  86.4 6.6 %collective-permute-start.5 = (bf16[128,2,1,128]{3,2,1,0:T(2,128)(2,1)S(1)}, bf16[128,2,1,128]{3,2,1,0:T(2,128)(2,1)S(1)}, u32[]{:S(2)}, u32[]{:S(2)}) collective-permute-start(bf16[128,2,1,128]{3,2,1,0:T(2,128)(2,1)S(1)} %get-tuple-element.34), channel_id=1, source_target_pairs={{2,0},{4,2},{6,4},{8,6},{10,8},{12,10},{14,12},{16,14},{18,16},{20... | collective-permute-start | bytes 196616 | tf_op jit(solution)/shard_map/ppermute | solution.py:17
  93.5 1.6 collective-permute-done.4
  95.1 1.5 collective-permute-done.5
  96.6 1.3 collective-permute-start.6
  97.9 3.0 collective-permute-start.7
  102.4 2.0 pad_maximum_fusion.1
  108.8 1.4 fusion.3
  110.2 10.4 %all-to-all-start.1 = ((bf16[128,2,16,128]{3,2,1,0:T(8,128)(2,1)}), bf16[128,2,16,128]{3,2,1,0:T(8,128)(2,1)}, u32[]{:S(2)}, u32[]{:S(2)}) async-start(bf16[128,2,16,128]{3,2,1,0:T(8,128)(2,1)} %bitcast.251), calls=%async_computation.1 | async-start | bytes 2097152 | tf_op jit(solution)/shard_map/all_to_all | solution.py:111
  120.9 1.8 convolution_bitcast_fusion.10
  127.7 23.3 %all-to-all-done.1 = bf16[128,2,16,128]{3,2,1,0:T(8,128)(2,1)} async-done(((bf16[128,2,16,128]{3,2,1,0:T(8,128)(2,1)}), bf16[128,2,16,128]{3,2,1,0:T(8,128)(2,1)}, u32[]{:S(2)}, u32[]{:S(2)}) %all-to-all-start.1) | async-done | bytes 1048608 | tf_op jit(solution)/shard_map/all_to_all | solution.py:111
  150.9 1.5 copy.12
  154.9 1.5 bitcast_multiply_fusion.2
  157.6 1.4 fusion.8
  159.1 244.5 %all-reduce.6.cloned.1.call-done = (f32[3,128,128]{2,1,0:T(8,128)}, f32[3,3,128,128]{3,2,1,0:T(8,128)}) async-done(((f32[3,128,128]{2,1,0:T(8,128)}, f32[3,3,128,128]{3,2,1,0:T(8,128)}), (f32[3,128,128]{2,1,0:T(8,128)}, f32[3,3,128,128]{3,2,1,0:T(8,128)})) %all-reduce.6.cloned.1.call-update) | async-done | bytes 786448 | tf_op jit(solution)/shard_map/psum | solution.py:137
  403.6 1.6 copy.18
  405.2 1.9 copy.19
  (110 shorter events, 31.7 us)
Async XLA Ops:
  7.2 3.1 copy-start.19
  10.2 1.8 copy-start.9
  10.2 1.6 copy-start.15
  60.2 9.0 %collective-permute-start = (bf16[128,2,1,128]{3,2,1,0:T(2,128)(2,1)S(1)}, bf16[128,2,1,128]{3,2,1,0:T(2,128)(2,1)S(1)}, u32[]{:S(2)}, u32[]{:S(2)}) collective-permute-start(bf16[128,2,1,128]{3,2,1,0:T(2,128)(2,1)S(1)} %get-tuple-element.37), channel_id=1, source_target_pairs={{0,2},{2,4},{4,6},{6,8},{8,10},{10,12},{12,14},{14,16},{16,18},{18... | collective-permute-start | bytes 196616 | tf_op jit(solution)/shard_map/ppermute | solution.py:15
  62.7 8.0 %collective-permute-start.1 = (bf16[128,2,1,128]{3,2,1,0:T(2,128)(2,1)S(1)}, bf16[128,2,1,128]{3,2,1,0:T(2,128)(2,1)S(1)}, u32[]{:S(2)}, u32[]{:S(2)}) collective-permute-start(bf16[128,2,1,128]{3,2,1,0:T(2,128)(2,1)S(1)} %get-tuple-element.38), channel_id=1, source_target_pairs={{2,0},{4,2},{6,4},{8,6},{10,8},{12,10},{14,12},{16,14},{18,16},{20... | collective-permute-start | bytes 196616 | tf_op jit(solution)/shard_map/ppermute | solution.py:17
  68.5 5.9 %copy-start.18 = (bf16[3,3,128,128]{3,2,1,0:T(8,128)(2,1)S(1)}, bf16[3,3,128,128]{3,2,1,0:T(8,128)(2,1)}, u32[]{:S(2)}) copy-start(bf16[3,3,128,128]{3,2,1,0:T(8,128)(2,1)} %param.9) | copy-start | bytes 884740
  70.7 4.1 collective-permute-start.2
  72.0 3.1 collective-permute-start.3
  74.4 8.0 %copy-start.16 = (bf16[128,2,16,128]{3,2,1,0:T(8,128)(2,1)}, bf16[128,2,16,128]{3,2,1,0:T(8,128)(2,1)S(1)}, u32[]{:S(2)}) copy-start(bf16[128,2,16,128]{3,2,1,0:T(8,128)(2,1)S(1)} %get-tuple-element.35) | copy-start | bytes 3145732
  78.5 1.4 copy-start.8
  78.5 1.8 copy-start.6
  78.5 2.2 copy-start.2
  78.5 3.0 copy-start.4
  84.4 10.6 %collective-permute-start.4 = (bf16[128,2,1,128]{3,2,1,0:T(2,128)(2,1)S(1)}, bf16[128,2,1,128]{3,2,1,0:T(2,128)(2,1)S(1)}, u32[]{:S(2)}, u32[]{:S(2)}) collective-permute-start(bf16[128,2,1,128]{3,2,1,0:T(2,128)(2,1)S(1)} %get-tuple-element.33), channel_id=1, source_target_pairs={{0,2},{2,4},{4,6},{6,8},{8,10},{10,12},{12,14},{14,16},{16,18},{18... | collective-permute-start | bytes 196616 | tf_op jit(solution)/shard_map/ppermute | solution.py:15
  86.4 10.2 %collective-permute-start.5 = (bf16[128,2,1,128]{3,2,1,0:T(2,128)(2,1)S(1)}, bf16[128,2,1,128]{3,2,1,0:T(2,128)(2,1)S(1)}, u32[]{:S(2)}, u32[]{:S(2)}) collective-permute-start(bf16[128,2,1,128]{3,2,1,0:T(2,128)(2,1)S(1)} %get-tuple-element.34), channel_id=1, source_target_pairs={{2,0},{4,2},{6,4},{8,6},{10,8},{12,10},{14,12},{16,14},{18,16},{20... | collective-permute-start | bytes 196616 | tf_op jit(solution)/shard_map/ppermute | solution.py:17
  96.6 5.8 %collective-permute-start.6 = (bf16[1,2,18,128]{3,2,1,0:T(8,128)(2,1)S(1)}, bf16[1,2,18,128]{3,2,1,0:T(8,128)(2,1)S(1)}, u32[]{:S(2)}, u32[]{:S(2)}) collective-permute-start(bf16[1,2,18,128]{3,2,1,0:T(8,128)(2,1)S(1)} %get-tuple-element.22), channel_id=1, source_target_pairs={{1,0},{3,2},{5,4},{7,6},{9,8},{11,10},{13,12},{15,14},{17,16},{19,... | collective-permute-start | bytes 27656 | tf_op jit(solution)/shard_map/ppermute | solution.py:17
  97.9 4.5 %collective-permute-start.7 = (bf16[1,2,18,128]{3,2,1,0:T(8,128)(2,1)S(1)}, bf16[1,2,18,128]{3,2,1,0:T(8,128)(2,1)S(1)}, u32[]{:S(2)}, u32[]{:S(2)}) collective-permute-start(bf16[1,2,18,128]{3,2,1,0:T(8,128)(2,1)S(1)} %get-tuple-element.23), channel_id=1, source_target_pairs={{0,1},{2,3},{4,5},{6,7},{8,9},{10,11},{12,13},{14,15},{16,17},{18,... | collective-permute-start | bytes 27656 | tf_op jit(solution)/shard_map/ppermute | solution.py:15
  110.2 40.7 %all-to-all-start.1 = ((bf16[128,2,16,128]{3,2,1,0:T(8,128)(2,1)}), bf16[128,2,16,128]{3,2,1,0:T(8,128)(2,1)}, u32[]{:S(2)}, u32[]{:S(2)}) async-start(bf16[128,2,16,128]{3,2,1,0:T(8,128)(2,1)} %bitcast.251), calls=%async_computation.1 | async-start | bytes 2097152 | tf_op jit(solution)/shard_map/all_to_all | solution.py:111
  120.6 282.9 %all-reduce.6.cloned.1.call-start = ((), (), s32[]{:S(2)}) async-start(), calls=%async_computation.2 | async-start | bytes 1572864 | tf_op jit(solution)/shard_map/psum | solution.py:137
  120.9 1.9 copy-start.7
  120.9 2.4 copy-start.5
  124.5 1.3 copy-start.1
  126.8 25.7 %copy-start.14 = (bf16[1,16,256,128]{3,2,1,0:T(8,128)(2,1)S(1)}, bf16[1,16,256,128]{3,2,1,0:T(8,128)(2,1)}, u32[]{:S(2)}) copy-start(bf16[1,16,256,128]{3,2,1,0:T(8,128)(2,1)} %copy-done.13) | copy-start | bytes 3145732
  150.9 2.0 copy-start.12
  (7 other events, 8.2 us)
Sparse Core Ops, SparseCore 0:
  155.1 248.4 all-reduce.5
where the time goes:
time: 415 us; the launch traced here: 414 us
  waiting for transfers between devices  273 us (66%)
  blocking collectives  46.1 us (11%)
  starting transfers between devices  34.1 us (8%)
  matrix products  20 us (5%)
  between operations  14.7 us (4%)
  local copies, waits for them, and re-layouts  13.4 us (3%)
  other arithmetic  12.4 us (3%)
    psum x1, waiting for transfers between devices, shards(): lax.psum((temporal_local * scale, spatial_local * scale), ('tm', 'height'...  245 us
    all_to_all x1, blocking collectives, shards(): lax.all_to_all(arranged, ('tm', 'height'), split_axis=0, concat_axis=0, t...  46.1 us
    all_to_all x1, waiting for transfers between devices, shards(): lax.all_to_all(grad_act_space, ('tm', 'height'), split_axis=0, concat_axi...  23.3 us
    ppermute x4, starting transfers between devices, with_halo(): lax.ppermute(head, axis, [((i + 1) % count, i) for i in range(ends)])  14.7 us
    all_to_all x1, starting transfers between devices, shards(): lax.all_to_all(grad_act_space, ('tm', 'height'), split_axis=0, concat_axi...  10.4 us
    ppermute x4, starting transfers between devices, with_halo(): lax.ppermute(tail, axis, [(i, (i + 1) % count) for i in range(ends)])  8.68 us
  transfers between devices with their start and end apart: 10, of which 7 were waited for; matrix products, arithmetic and copies ran while one was open for 3% of the time, Pallas kernels for 0%

commit v1 on v0

--- a/solution.py
+++ b/solution.py
@@ -135,7 +135,7 @@
     video_grad = frame_total.astype(jnp.bfloat16)[None]
     scale = float(frames * rows * total_cols) ** (-0.5)
     temporal_grad, spatial_grad = lax.psum(
-        (temporal_local * scale, spatial_local * scale), ("tm", "height", "width")
+        lax.psum((temporal_local * scale, spatial_local * scale), "tm"), ("height", "width")
     )
     return (video_grad, temporal_grad, spatial_grad)
 

time: 415 us -> 352 us (0.85)
  waiting for transfers between devices: 273 us -> 209 us
    psum x1 -> x2, waiting for transfers between devices: 245 us -> 180 us  [the longest x1 113 us: shards(): lax.psum(lax.psum((temporal_local * scale, spatial_local * scale), 'tm'),...]
  transfers between devices with their start and end apart: 10 -> 11, of which waited for: 7 -> 8; matrix products, arithmetic and copies ran while one was open for 3% -> 4% of each run, Pallas kernels for 0% -> 0%
where the time goes in v1:
time: 352 us; the launch traced here: 350 us
  waiting for transfers between devices  209 us (59%)
  blocking collectives  46.1 us (13%)
  starting transfers between devices  34.3 us (10%)
  matrix products  19.9 us (6%)
  between operations  14.7 us (4%)
  local copies, waits for them, and re-layouts  13.5 us (4%)
  other arithmetic  12.4 us (4%)
    psum x1, waiting for transfers between devices, shards(): lax.psum(lax.psum((temporal_local * scale, spatial_local * scale), 'tm'),...  113 us
    psum x1, waiting for transfers between devices, shards(): lax.psum((temporal_local * scale, spatial_local * scale), 'tm')  67 us
    all_to_all x1, blocking collectives, shards(): lax.all_to_all(arranged, ('tm', 'height'), split_axis=0, concat_axis=0, t...  46.1 us
    all_to_all x1, waiting for transfers between devices, shards(): lax.all_to_all(grad_act_space, ('tm', 'height'), split_axis=0, concat_axi...  23.3 us
    ppermute x4, starting transfers between devices, with_halo(): lax.ppermute(head, axis, [((i + 1) % count, i) for i in range(ends)])  14.9 us
    all_to_all x1, starting transfers between devices, shards(): lax.all_to_all(grad_act_space, ('tm', 'height'), split_axis=0, concat_axi...  10.4 us
    ppermute x4, starting transfers between devices, with_halo(): lax.ppermute(tail, axis, [(i, (i + 1) % count) for i in range(ends)])  8.68 us
    unnamed x44, local copies, waits for them, and re-layouts  8.11 us
  transfers between devices with their start and end apart: 11, of which 8 were waited for; matrix products, arithmetic and copies ran while one was open for 4% of the time, Pallas kernels for 0%

profile of v1, /device:TPU:2, one launch (start us, length us, event | category | flops | bytes accessed | tf_op | source)
XLA Modules:
  0.0 349.8 jit_solution(8325672010279623250)
XLA Ops:
  8.8 1.4 broadcast_multiply_fusion
  14.0 46.1 %all_to_all.10 = bf16[128,2,16,128]{3,2,1,0:T(8,128)(2,1)S(1)} all-to-all(bf16[128,2,16,128]{3,2,1,0:T(8,128)(2,1)S(1)} %bitcast.249), channel_id=1, replica_groups=mesh['tm'=8,'height'=16,'width'=2] {'tm','height'}, dimensions={0} | all-to-all | bytes 2097152 | tf_op jit(solution)/shard_map/all_to_all | solution.py:79
  60.2 2.4 collective-permute-start
  62.7 5.6 %collective-permute-start.1 = (bf16[128,2,1,128]{3,2,1,0:T(2,128)(2,1)S(1)}, bf16[128,2,1,128]{3,2,1,0:T(2,128)(2,1)S(1)}, u32[]{:S(2)}, u32[]{:S(2)}) collective-permute-start(bf16[128,2,1,128]{3,2,1,0:T(2,128)(2,1)S(1)} %get-tuple-element.40), channel_id=1, source_target_pairs={{2,0},{4,2},{6,4},{8,6},{10,8},{12,10},{14,12},{16,14},{18,16},{20... | collective-permute-start | bytes 196616 | tf_op jit(solution)/shard_map/ppermute | solution.py:17
  69.2 1.6 collective-permute-done.1
  75.2 2.0 maximum_maximum_fusion
  77.2 1.3 fusion.67
  84.6 1.9 collective-permute-start.4
  86.5 6.6 %collective-permute-start.5 = (bf16[128,2,1,128]{3,2,1,0:T(2,128)(2,1)S(1)}, bf16[128,2,1,128]{3,2,1,0:T(2,128)(2,1)S(1)}, u32[]{:S(2)}, u32[]{:S(2)}) collective-permute-start(bf16[128,2,1,128]{3,2,1,0:T(2,128)(2,1)S(1)} %get-tuple-element.36), channel_id=1, source_target_pairs={{2,0},{4,2},{6,4},{8,6},{10,8},{12,10},{14,12},{16,14},{18,16},{20... | collective-permute-start | bytes 196616 | tf_op jit(solution)/shard_map/ppermute | solution.py:17
  93.7 1.6 collective-permute-done.4
  95.2 1.5 collective-permute-done.5
  98.1 3.0 collective-permute-start.7
  102.6 2.0 pad_maximum_fusion.1
  108.9 1.4 fusion.3
  110.4 10.4 %all-to-all-start.1 = ((bf16[128,2,16,128]{3,2,1,0:T(8,128)(2,1)}), bf16[128,2,16,128]{3,2,1,0:T(8,128)(2,1)}, u32[]{:S(2)}, u32[]{:S(2)}) async-start(bf16[128,2,16,128]{3,2,1,0:T(8,128)(2,1)} %bitcast.251), calls=%async_computation.1 | async-start | bytes 2097152 | tf_op jit(solution)/shard_map/all_to_all | solution.py:111
  121.1 1.8 convolution_bitcast_fusion.10
  127.8 23.3 %all-to-all-done.1 = bf16[128,2,16,128]{3,2,1,0:T(8,128)(2,1)} async-done(((bf16[128,2,16,128]{3,2,1,0:T(8,128)(2,1)}), bf16[128,2,16,128]{3,2,1,0:T(8,128)(2,1)}, u32[]{:S(2)}, u32[]{:S(2)}) %all-to-all-start.1) | async-done | bytes 1048608 | tf_op jit(solution)/shard_map/all_to_all | solution.py:111
  151.1 1.5 copy.12
  155.4 1.5 bitcast_multiply_fusion.2
  156.9 67.0 %all-reduce.10.cloned.1.call-done = (f32[3,128,128]{2,1,0:T(8,128)}, f32[3,3,128,128]{3,2,1,0:T(8,128)}) async-done(((f32[3,128,128]{2,1,0:T(8,128)}, f32[3,3,128,128]{3,2,1,0:T(8,128)}), (f32[3,128,128]{2,1,0:T(8,128)}, f32[3,3,128,128]{3,2,1,0:T(8,128)})) %all-reduce.10.cloned.1.call-update) | async-done | bytes 786448 | tf_op jit(solution)/shard_map/psum | solution.py:138
  225.1 1.4 fusion.8
  226.5 112.9 %all-reduce.8.cloned.1.call-done = (f32[3,128,128]{2,1,0:T(8,128)}, f32[3,3,128,128]{3,2,1,0:T(8,128)}) async-done(((f32[3,128,128]{2,1,0:T(8,128)}, f32[3,3,128,128]{3,2,1,0:T(8,128)}), (f32[3,128,128]{2,1,0:T(8,128)}, f32[3,3,128,128]{3,2,1,0:T(8,128)})) %all-reduce.8.cloned.1.call-update) | async-done | bytes 786448 | tf_op jit(solution)/shard_map/psum | solution.py:137
  339.4 1.6 copy.20
  341.0 1.9 copy.21
  (113 shorter events, 33.2 us)
Async XLA Ops:
  7.2 3.1 copy-start.19
  10.2 1.8 copy-start.9
  10.2 1.6 copy-start.15
  60.2 9.0 %collective-permute-start = (bf16[128,2,1,128]{3,2,1,0:T(2,128)(2,1)S(1)}, bf16[128,2,1,128]{3,2,1,0:T(2,128)(2,1)S(1)}, u32[]{:S(2)}, u32[]{:S(2)}) collective-permute-start(bf16[128,2,1,128]{3,2,1,0:T(2,128)(2,1)S(1)} %get-tuple-element.39), channel_id=1, source_target_pairs={{0,2},{2,4},{4,6},{6,8},{8,10},{10,12},{12,14},{14,16},{16,18},{18... | collective-permute-start | bytes 196616 | tf_op jit(solution)/shard_map/ppermute | solution.py:15
  62.7 11.8 %copy-start.18 = (bf16[3,3,128,128]{3,2,1,0:T(8,128)(2,1)S(1)}, bf16[3,3,128,128]{3,2,1,0:T(8,128)(2,1)}, u32[]{:S(2)}) copy-start(bf16[3,3,128,128]{3,2,1,0:T(8,128)(2,1)} %param.9) | copy-start | bytes 884740
  62.7 8.1 %collective-permute-start.1 = (bf16[128,2,1,128]{3,2,1,0:T(2,128)(2,1)S(1)}, bf16[128,2,1,128]{3,2,1,0:T(2,128)(2,1)S(1)}, u32[]{:S(2)}, u32[]{:S(2)}) collective-permute-start(bf16[128,2,1,128]{3,2,1,0:T(2,128)(2,1)S(1)} %get-tuple-element.40), channel_id=1, source_target_pairs={{2,0},{4,2},{6,4},{8,6},{10,8},{12,10},{14,12},{16,14},{18,16},{20... | collective-permute-start | bytes 196616 | tf_op jit(solution)/shard_map/ppermute | solution.py:17
  70.9 4.1 %collective-permute-start.2 = (bf16[1,2,18,128]{3,2,1,0:T(8,128)(2,1)S(1)}, bf16[1,2,18,128]{3,2,1,0:T(8,128)(2,1)S(1)}, u32[]{:S(2)}, u32[]{:S(2)}) collective-permute-start(bf16[1,2,18,128]{3,2,1,0:T(8,128)(2,1)S(1)} %get-tuple-element.28), channel_id=1, source_target_pairs={{0,1},{2,3},{4,5},{6,7},{8,9},{10,11},{12,13},{14,15},{16,17},{18,... | collective-permute-start | bytes 27656 | tf_op jit(solution)/shard_map/ppermute | solution.py:15
  72.2 3.1 collective-permute-start.3
  74.5 8.0 %copy-start.16 = (bf16[128,2,16,128]{3,2,1,0:T(8,128)(2,1)}, bf16[128,2,16,128]{3,2,1,0:T(8,128)(2,1)S(1)}, u32[]{:S(2)}) copy-start(bf16[128,2,16,128]{3,2,1,0:T(8,128)(2,1)S(1)} %get-tuple-element.37) | copy-start | bytes 3145732
  78.6 1.4 copy-start.8
  78.6 1.8 copy-start.6
  78.6 2.2 copy-start.2
  78.6 3.0 copy-start.4
  84.6 10.6 %collective-permute-start.4 = (bf16[128,2,1,128]{3,2,1,0:T(2,128)(2,1)S(1)}, bf16[128,2,1,128]{3,2,1,0:T(2,128)(2,1)S(1)}, u32[]{:S(2)}, u32[]{:S(2)}) collective-permute-start(bf16[128,2,1,128]{3,2,1,0:T(2,128)(2,1)S(1)} %get-tuple-element.35), channel_id=1, source_target_pairs={{0,2},{2,4},{4,6},{6,8},{8,10},{10,12},{12,14},{14,16},{16,18},{18... | collective-permute-start | bytes 196616 | tf_op jit(solution)/shard_map/ppermute | solution.py:15
  86.5 10.2 %collective-permute-start.5 = (bf16[128,2,1,128]{3,2,1,0:T(2,128)(2,1)S(1)}, bf16[128,2,1,128]{3,2,1,0:T(2,128)(2,1)S(1)}, u32[]{:S(2)}, u32[]{:S(2)}) collective-permute-start(bf16[128,2,1,128]{3,2,1,0:T(2,128)(2,1)S(1)} %get-tuple-element.36), channel_id=1, source_target_pairs={{2,0},{4,2},{6,4},{8,6},{10,8},{12,10},{14,12},{16,14},{18,16},{20... | collective-permute-start | bytes 196616 | tf_op jit(solution)/shard_map/ppermute | solution.py:17
  96.8 5.8 %collective-permute-start.6 = (bf16[1,2,18,128]{3,2,1,0:T(8,128)(2,1)S(1)}, bf16[1,2,18,128]{3,2,1,0:T(8,128)(2,1)S(1)}, u32[]{:S(2)}, u32[]{:S(2)}) collective-permute-start(bf16[1,2,18,128]{3,2,1,0:T(8,128)(2,1)S(1)} %get-tuple-element.24), channel_id=1, source_target_pairs={{1,0},{3,2},{5,4},{7,6},{9,8},{11,10},{13,12},{15,14},{17,16},{19,... | collective-permute-start | bytes 27656 | tf_op jit(solution)/shard_map/ppermute | solution.py:17
  98.1 4.5 %collective-permute-start.7 = (bf16[1,2,18,128]{3,2,1,0:T(8,128)(2,1)S(1)}, bf16[1,2,18,128]{3,2,1,0:T(8,128)(2,1)S(1)}, u32[]{:S(2)}, u32[]{:S(2)}) collective-permute-start(bf16[1,2,18,128]{3,2,1,0:T(8,128)(2,1)S(1)} %get-tuple-element.25), channel_id=1, source_target_pairs={{0,1},{2,3},{4,5},{6,7},{8,9},{10,11},{12,13},{14,15},{16,17},{18,... | collective-permute-start | bytes 27656 | tf_op jit(solution)/shard_map/ppermute | solution.py:15
  110.4 40.7 %all-to-all-start.1 = ((bf16[128,2,16,128]{3,2,1,0:T(8,128)(2,1)}), bf16[128,2,16,128]{3,2,1,0:T(8,128)(2,1)}, u32[]{:S(2)}, u32[]{:S(2)}) async-start(bf16[128,2,16,128]{3,2,1,0:T(8,128)(2,1)} %bitcast.251), calls=%async_computation.1 | async-start | bytes 2097152 | tf_op jit(solution)/shard_map/all_to_all | solution.py:111
  120.8 103.1 %all-reduce.10.cloned.1.call-start = ((), (), s32[]{:S(2)}) async-start(), calls=%async_computation.3 | async-start | bytes 1572864 | tf_op jit(solution)/shard_map/psum | solution.py:138
  121.1 1.9 copy-start.7
  121.1 2.4 copy-start.5
  126.9 25.7 %copy-start.14 = (bf16[1,16,256,128]{3,2,1,0:T(8,128)(2,1)S(1)}, bf16[1,16,256,128]{3,2,1,0:T(8,128)(2,1)}, u32[]{:S(2)}) copy-start(bf16[1,16,256,128]{3,2,1,0:T(8,128)(2,1)} %copy-done.13) | copy-start | bytes 3145732
  151.1 2.0 copy-start.12
  155.1 184.3 %all-reduce.8.cloned.1.call-start = ((), (), s32[]{:S(2)}) async-start(), calls=%async_computation.2 | async-start | bytes 1572864 | tf_op jit(solution)/shard_map/psum | solution.py:137
  (8 other events, 9.5 us)
Sparse Core Ops, SparseCore 0:
  155.2 68.6 all-reduce.9
  227.5 111.8 all-reduce.7
